TPU v7x, 512 devices: a whole 4x4x16 slice. The times are simulated.
512 devices in a mesh: vocab: 16 (over z_hi, y, core), dp: 8 (over z_lo), replica: 4 (over x).
Axes of the slice: x: 4, y: 4, z: 16 (z_hi: 2, z_lo: 8; z = z_hi * 8 + z_lo), core: 2. Of those that a mesh axis runs over, the one named last changes fastest.
Arguments:
- hidden: bfloat16 [1024, 4096], P('dp'), may hold values from -6 to 6
- head_weight: bfloat16 [4096, 65536], P('dp', ('vocab', 'replica')), may hold values from -0.09375 to 0.09375
- head_bias: float32 [65536], P(('vocab', 'replica')), may hold values from -2.5 to 2.5
- rep_cotangent: float32 [64, 65536], P('dp', ('vocab', 'replica')), may hold values from -6 to 6
- lengths: int32 [64], P('dp'), may hold values from 1 to 16, 640 in all
Outputs:
- pooled: float32 [64, 65536], P('dp', ('vocab', 'replica'))
- term_mean: float32 [65536], P(('vocab', 'replica'))
- bias_grad: float32 [65536], P(('vocab', 'replica'))
- weight_grad: float32 [4096, 65536], P('dp', ('vocab', 'replica'))
- input_grad: float32 [1024, 4096], P(('vocab', 'replica'), 'dp')
Inputs may be any that keep to these rules, and one draw needn't show every extreme that they name: `lengths`: each sequence has at least one live token; some sequence has all 16 live.
All inputs are finite; a program needn't handle non-finite values. No bound on the sum of `lengths` on one device may be relied on, other than what follows from the above.
Results may differ from a plain program's by a relative error of at most 0.015.
Values may be sent and summed in bfloat16 or wider, within the bound.
No kernel may reach another device: no remote copies, remote signals or barrier semaphores. Data moves between devices by JAX's collectives and lax.ppermute only.
A program may use at most 64 MiB of HBM per device.

v0:
```python
import jax
import jax.numpy as jnp
from jax import lax
from jax.sharding import PartitionSpec as P


def per_device(hidden, head_weight, head_bias, rep_cotangent, lengths):
    tok_rows = hidden.shape[0]
    block = head_weight.shape[0]
    vocab_cols = head_weight.shape[1]
    dp_count = lax.axis_size("dp")
    seq_count = lengths.shape[0]
    seq_len = tok_rows // seq_count
    columns = lax.all_to_all(hidden, "dp", split_axis=1, concat_axis=0, tiled=True)
    running = jnp.zeros((tok_rows, vocab_cols), jnp.float32)
    piece = lax.all_gather(head_weight, "dp", axis=0, tiled=True)
    count = piece.shape[0] // block
    for index in range(count):
        left = lax.dynamic_slice_in_dim(hidden, index * block, block, 1)
        part = jnp.dot(
            left, piece[index * block : (index + 1) * block, :], preferred_element_type=jnp.float32
        ).astype(jnp.bfloat16)
        running = running + lax.optimization_barrier(part).astype(jnp.float32)
    logits = running + head_bias[None, :]
    positive = jnp.maximum(logits, 0.0)
    grid = jnp.log1p(positive).reshape(seq_count, seq_len, vocab_cols)
    live = (jnp.arange(seq_len, dtype=jnp.int32)[None, :] < lengths[:, None]).astype(jnp.float32)[
        :, :, None
    ]
    squared = grid * grid
    total = 1.0 + jnp.sum(live * squared * squared, axis=1)
    pooled = total**0.25 - 1.0
    factor = (
        live
        * squared
        * grid
        * (total ** (-0.75))[:, None, :]
        / (1.0 + positive.reshape(seq_count, seq_len, vocab_cols))
    )
    column_sum = jnp.sum(pooled, axis=0)
    seq_total = seq_count * dp_count
    term_mean = lax.psum(column_sum, "dp") / seq_total
    grad_pooled = rep_cotangent + term_mean[None, :]
    grad_logits = (factor * grad_pooled[:, None, :]).reshape(tok_rows, vocab_cols)
    bias_grad = lax.psum(jnp.sum(grad_logits, axis=0), "dp")
    grad_round = grad_logits.astype(jnp.bfloat16)
    piece = lax.all_gather(grad_round, "dp", axis=0, tiled=True)
    left = columns
    weight_sum_acc = jnp.einsum("tk,tv->kv", left, piece, preferred_element_type=jnp.float32)
    rows_out = jnp.einsum("tv,kv->tk", piece, head_weight, preferred_element_type=jnp.float32)
    input_part = rows_out
    weight_grad, input_part = (weight_sum_acc, input_part)
    input_grad = lax.psum_scatter(input_part, ("vocab", "replica"), scatter_dimension=0, tiled=True)
    return (pooled, term_mean, bias_grad, weight_grad, input_grad)


def solution(mesh):
    placed = (
        P("dp", None),
        P("dp", ("vocab", "replica")),
        P(("vocab", "replica")),
        P("dp", ("vocab", "replica")),
        P("dp"),
    )
    return jax.shard_map(
        per_device,
        mesh=mesh,
        in_specs=placed,
        out_specs=(
            P("dp", ("vocab", "replica")),
            P(("vocab", "replica")),
            P(("vocab", "replica")),
            P("dp", ("vocab", "replica")),
            P(("vocab", "replica"), "dp"),
        ),
        check_vma=False,
    )
```

profile of v0, /device:TPU:64, one launch (start us, length us, event | category | flops | bytes accessed | tf_op | source)
XLA Modules:
  0.0 897.8 jit_solution(8657482168924879488)
XLA Ops:
  7.2 0.0 copy-start.3
  7.2 0.0 copy-start.1
  7.2 0.0 all-gather.3.cloned.1.call-start
  7.2 0.7 all-gather.3.cloned.1.call-update
  7.9 0.0 all-gather.5.cloned.1.call-start
  8.0 0.7 fusion.18
  8.7 0.1 reshape.55
  8.8 0.0 copy-start
  8.8 180.1 %all-gather.3.cloned.1.call-done = bf16[4096,1024]{1,0:T(8,128)(2,1)} async-done(((bf16[512,1024]{1,0:T(8,128)(2,1)}), bf16[4096,1024]{1,0:T(8,128)(2,1)}) %all-gather.3.cloned.1.call-update) | async-done | bytes 8388624 | tf_op jit(solution)/shard_map/all_gather | solution.py:16
  188.9 1.6 convolution_convert_fusion.7
  190.5 1.6 convolution_convert_fusion.6
  192.1 1.6 convolution_convert_fusion.5
  193.7 1.6 convolution_convert_fusion.4
  195.4 1.6 convolution_convert_fusion.3
  197.0 1.6 convolution_convert_fusion.2
  198.6 1.6 convolution_convert_fusion.1
  200.2 1.6 convolution_convert_fusion
  201.9 0.0 copy-done.3
  201.9 0.6 fusion.8
  202.5 0.6 fusion.20
  203.1 26.0 %psum.14 = f32[1024]{0:T(1024)S(1)} all-reduce(f32[1024]{0:T(1024)S(1)} %get-tuple-element.22), channel_id=1, replica_groups=mesh['vocab'=16,'dp'=8,'replica'=4] {'dp'}, use_global_device_ids=true, to_apply=%region_2.0 | all-reduce | flops 1024 | bytes 8192 | tf_op jit(solution)/shard_map/psum | solution.py:42
  229.1 0.0 copy-done.1
  229.1 0.0 copy-start.2
  229.1 1.0 fusion.19
  230.1 0.0 all-gather.5.cloned.1.call-update
  230.1 0.0 reduce-scatter.2.cloned.1.call-start
  230.2 73.2 %all-gather.5.cloned.1.call-done = bf16[1024,1024]{1,0:T(8,128)(2,1)} async-done(((bf16[128,1024]{1,0:T(8,128)(2,1)}), bf16[1024,1024]{1,0:T(8,128)(2,1)}) %all-gather.5.cloned.1.call-update) | async-done | bytes 2097168 | tf_op jit(solution)/shard_map/all_gather | solution.py:47
  303.4 0.0 copy-done
  303.4 4.2 fusion.21
  307.5 0.0 reduce-scatter.2.cloned.1.call-update
  307.6 1.6 copy.12
  309.2 59.9 %all_to_all.19 = bf16[128,8,512]{0,2,1:T(8,128)(2,1)S(1)} all-to-all(bf16[128,8,512]{0,2,1:T(8,128)(2,1)S(1)} %bitcast.22), channel_id=1, replica_groups=mesh['vocab'=16,'dp'=8,'replica'=4] {'dp'}, dimensions={1} | all-to-all | bytes 2097152 | tf_op jit(solution)/shard_map/all_to_all | solution.py:14
  369.1 0.0 copy-done.2
  369.1 0.5 copy.13
  369.7 23.8 %psum.15 = f32[1024]{0:T(1024)} all-reduce(f32[1024]{0:T(1024)S(1)} %reduce_sum.29), channel_id=1, replica_groups=mesh['vocab'=16,'dp'=8,'replica'=4] {'dp'}, use_global_device_ids=true, to_apply=%region_4.0 | all-reduce | flops 1024 | bytes 8192 | tf_op jit(solution)/shard_map/psum | solution.py:45
  393.5 2.9 convolution_bitcast_fusion
  396.4 1.8 copy.14
  398.2 493.1 %reduce-scatter.2.cloned.1.call-done = f32[16,512]{1,0:T(8,128)} async-done(((f32[1024,512]{1,0:T(8,128)}), f32[16,512]{1,0:T(8,128)}) %reduce-scatter.2.cloned.1.call-update) | async-done | bytes 32784 | tf_op jit(solution)/shard_map/reduce_scatter | solution.py:53
  (3 shorter events, 0.1 us)
Async XLA Ops:
  7.2 194.7 %copy-start.3 = (f32[1024]{0:T(1024)S(1)}, f32[1024]{0:T(1024)}, u32[]{:S(2)}) copy-start(f32[1024]{0:T(1024)} %param.7) | copy-start | bytes 12292
  7.2 221.9 %copy-start.1 = (f32[8,1024]{1,0:T(8,128)S(1)}, f32[8,1024]{1,0:T(8,128)}, u32[]{:S(2)}) copy-start(f32[8,1024]{1,0:T(8,128)} %param.8) | copy-start | bytes 98308
  7.2 181.7 %all-gather.3.cloned.1.call-start = ((), (), s32[]{:S(2)}) async-start(), calls=%async_computation.2 | async-start | bytes 9437184 | tf_op jit(solution)/shard_map/all_gather | solution.py:16
  7.9 295.4 %all-gather.5.cloned.1.call-start = ((), (), s32[]{:S(2)}) async-start(), calls=%async_computation.3 | async-start | bytes 2359296 | tf_op jit(solution)/shard_map/all_gather | solution.py:47
  8.8 294.6 %copy-start = (bf16[512,1024]{1,0:T(8,128)(2,1)S(1)}, bf16[512,1024]{1,0:T(8,128)(2,1)}, u32[]{:S(2)}) copy-start(bf16[512,1024]{1,0:T(8,128)(2,1)} %param.6) | copy-start | bytes 3145732
  229.1 140.0 %copy-start.2 = (f32[1024]{0:T(1024)}, f32[1024]{0:T(1024)S(1)}, u32[]{:S(2)}) copy-start(f32[1024]{0:T(1024)S(1)} %broadcast_multiply_fusion) | copy-start | bytes 12292
  230.1 661.1 %reduce-scatter.2.cloned.1.call-start = ((), (), s32[]{:S(2)}) async-start(), calls=%async_computation.4 | async-start | bytes 2129920 | tf_op jit(solution)/shard_map/reduce_scatter | solution.py:53
Sparse Core Ops, SparseCore 0:
  10.1 178.7 all-gather.2
  230.3 73.0 all-gather.4
  307.7 583.5 reduce-scatter.1
where the time goes:
time: 898 us
  waiting for transfers between devices  747 us (83%)
  blocking collectives  110 us (12%)
  matrix products  20 us (2%)
  between operations  13.9 us (2%)
    reduce_scatter x1, waiting for transfers between devices, per_device(): lax.psum_scatter(input_part, ('vocab', 'replica'), scatter_dimension=0, t...  493 us
    all_gather x1, waiting for transfers between devices, per_device(): piece = lax.all_gather(head_weight, 'dp', axis=0, tiled=True)  180 us
    all_gather x1, waiting for transfers between devices, per_device(): piece = lax.all_gather(grad_round, 'dp', axis=0, tiled=True)  73.2 us
    all_to_all x1, blocking collectives, per_device(): lax.all_to_all(hidden, 'dp', split_axis=1, concat_axis=0, tiled=True)  59.9 us
    psum x1, blocking collectives, per_device(): term_mean = lax.psum(column_sum, 'dp') / seq_total  26 us
    psum x1, blocking collectives, per_device(): bias_grad = lax.psum(jnp.sum(grad_logits, axis=0), 'dp')  23.8 us
  transfers between devices with their start and end apart: 3, of which 3 were waited for; matrix products, arithmetic and copies ran while one was open for 1% of the time, Pallas kernels for 0%

commit v1 on v0

--- a/solution.py
+++ b/solution.py
@@ -2,6 +2,11 @@
 import jax.numpy as jnp
 from jax import lax
 from jax.sharding import PartitionSpec as P
+
+
+def gather_over(array, mesh_axis, dim):
+    sent = jnp.stack([array] * lax.axis_size(mesh_axis))
+    return jnp.concatenate(lax.all_to_all(sent, mesh_axis, 0, 0), axis=dim)
 
 
 def per_device(hidden, head_weight, head_bias, rep_cotangent, lengths):
@@ -44,7 +49,7 @@
     grad_logits = (factor * grad_pooled[:, None, :]).reshape(tok_rows, vocab_cols)
     bias_grad = lax.psum(jnp.sum(grad_logits, axis=0), "dp")
     grad_round = grad_logits.astype(jnp.bfloat16)
-    piece = lax.all_gather(grad_round, "dp", axis=0, tiled=True)
+    piece = gather_over(grad_round, "dp", 0)
     left = columns
     weight_sum_acc = jnp.einsum("tk,tv->kv", left, piece, preferred_element_type=jnp.float32)
     rows_out = jnp.einsum("tv,kv->tk", piece, head_weight, preferred_element_type=jnp.float32)

time: 898 us -> 935 us (1.041)
  the two profiles are of different devices: /device:TPU:64 before, /device:TPU:160 now
where the time goes in v1:
time: 935 us; the launch traced here: 934 us
  waiting for transfers between devices  699 us (75%)
  blocking collectives  177 us (19%)
  matrix products  19.8 us (2%)
  between operations  14.2 us (2%)
  starting transfers between devices  10.7 us (1%)
    reduce_scatter x1, waiting for transfers between devices, per_device(): lax.psum_scatter(input_part, ('vocab', 'replica'), scatter_dimension=0, t...  519 us
    all_gather x1, waiting for transfers between devices, per_device(): piece = lax.all_gather(head_weight, 'dp', axis=0, tiled=True)  180 us
    all_to_all x1, blocking collectives, gather_over(): return jnp.concatenate(lax.all_to_all(sent, mesh_axis, 0, 0), axis=dim)  103 us
    psum x1, blocking collectives, per_device(): bias_grad = lax.psum(jnp.sum(grad_logits, axis=0), 'dp')  55.8 us
  transfers between devices with their start and end apart: 3, of which 2 were waited for; matrix products, arithmetic and copies ran while one was open for 1% of the time, Pallas kernels for 0%

profile of v1, /device:TPU:160, one launch (start us, length us, event | category | flops | bytes accessed | tf_op | source)
XLA Modules:
  0.0 934.3 jit_solution(10259096070349075655)
XLA Ops:
  7.2 0.0 copy-start.3
  7.2 0.0 copy-start.1
  7.2 0.0 all-gather.2.cloned.1.call-start
  7.2 0.7 all-gather.2.cloned.1.call-update
  7.9 0.0 reduce-scatter.2.cloned.1.call-start
  8.0 0.7 fusion.19
  8.7 0.1 reshape.61
  8.8 180.0 %all-gather.2.cloned.1.call-done = bf16[4096,1024]{1,0:T(8,128)(2,1)} async-done(((bf16[512,1024]{1,0:T(8,128)(2,1)}), bf16[4096,1024]{1,0:T(8,128)(2,1)}) %all-gather.2.cloned.1.call-update) | async-done | bytes 8388624 | tf_op jit(solution)/shard_map/all_gather | solution.py:21
  188.8 1.6 convolution_convert_fusion.7
  190.4 1.6 convolution_convert_fusion.6
  192.1 1.6 convolution_convert_fusion.5
  193.7 1.6 convolution_convert_fusion.4
  195.3 1.6 convolution_convert_fusion.3
  196.9 1.6 convolution_convert_fusion.2
  198.6 1.6 convolution_convert_fusion.1
  200.2 0.0 copy-start
  200.2 1.7 convolution_convert_fusion
  201.9 0.0 copy-done.3
  201.9 0.6 fusion.9
  202.5 0.6 fusion.21
  203.1 18.7 %psum.14 = f32[1024]{0:T(1024)S(1)} all-reduce(f32[1024]{0:T(1024)S(1)} %get-tuple-element.17), channel_id=1, replica_groups=mesh['vocab'=16,'dp'=8,'replica'=4] {'dp'}, use_global_device_ids=true, to_apply=%region_2.0 | all-reduce | flops 1024 | bytes 8192 | tf_op jit(solution)/shard_map/psum | solution.py:47
  221.8 0.0 copy-done.1
  221.9 0.0 copy-start.2
  221.9 1.1 fusion.20
  223.0 0.2 copy.12
  223.1 0.3 stack.2
  223.4 102.7 %all_to_all.21 = bf16[8,128,1024]{1,2,0:T(8,128)(2,1)S(1)} all-to-all(bf16[8,128,1024]{1,2,0:T(8,128)(2,1)S(1)} %stack.2), channel_id=1, replica_groups=mesh['vocab'=16,'dp'=8,'replica'=4] {'dp'}, dimensions={0} | all-to-all | bytes 4194304 | tf_op jit(solution)/shard_map/all_to_all | solution.py:9
  326.1 2.6 copy.15
  328.7 0.0 copy-done
  328.7 4.2 fusion.22
  332.9 0.0 copy-done.2
  332.9 0.0 reduce-scatter.2.cloned.1.call-update
  332.9 1.6 copy.13
  334.6 1.3 copy.14
  335.9 10.6 %all-to-all-start.1 = ((bf16[128,8,512]{2,0,1:T(8,128)(2,1)}), bf16[128,8,512]{2,0,1:T(8,128)(2,1)S(1)}, u32[]{:S(2)}, u32[]{:S(2)}) async-start(bf16[128,8,512]{2,0,1:T(8,128)(2,1)} %copy.14), calls=%async_computation.1 | async-start | bytes 2097152 | tf_op jit(solution)/shard_map/all_to_all | solution.py:19
  346.5 1.1 reduce_sum.29
  347.6 55.8 %psum.15 = f32[1024]{0:T(1024)} all-reduce(f32[1024]{0:T(1024)S(1)} %reduce_sum.29), channel_id=1, replica_groups=mesh['vocab'=16,'dp'=8,'replica'=4] {'dp'}, use_global_device_ids=true, to_apply=%region_4.0 | all-reduce | flops 1024 | bytes 8192 | tf_op jit(solution)/shard_map/psum | solution.py:50
  403.4 0.0 all-to-all-done.1
  403.4 2.5 convolution_bitcast_fusion
  405.9 2.9 copy.16
  408.8 518.7 %reduce-scatter.2.cloned.1.call-done = f32[16,512]{1,0:T(8,128)} async-done(((f32[1024,512]{1,0:T(8,128)}), f32[16,512]{1,0:T(8,128)}) %reduce-scatter.2.cloned.1.call-update) | async-done | bytes 32784 | tf_op jit(solution)/shard_map/reduce_scatter | solution.py:58
  (2 shorter events, 0.0 us)
Async XLA Ops:
  7.2 194.7 %copy-start.3 = (f32[1024]{0:T(1024)S(1)}, f32[1024]{0:T(1024)}, u32[]{:S(2)}) copy-start(f32[1024]{0:T(1024)} %param.7) | copy-start | bytes 12292
  7.2 214.7 %copy-start.1 = (f32[8,1024]{1,0:T(8,128)S(1)}, f32[8,1024]{1,0:T(8,128)}, u32[]{:S(2)}) copy-start(f32[8,1024]{1,0:T(8,128)} %param.8) | copy-start | bytes 98308
  7.2 181.6 %all-gather.2.cloned.1.call-start = ((), (), s32[]{:S(2)}) async-start(), calls=%async_computation.3 | async-start | bytes 9437184 | tf_op jit(solution)/shard_map/all_gather | solution.py:21
  7.9 919.6 %reduce-scatter.2.cloned.1.call-start = ((), (), s32[]{:S(2)}) async-start(), calls=%async_computation.4 | async-start | bytes 2129920 | tf_op jit(solution)/shard_map/reduce_scatter | solution.py:58
  200.2 128.5 %copy-start = (bf16[512,1024]{1,0:T(8,128)(2,1)S(1)}, bf16[512,1024]{1,0:T(8,128)(2,1)}, u32[]{:S(2)}) copy-start(bf16[512,1024]{1,0:T(8,128)(2,1)} %param.6) | copy-start | bytes 3145732
  221.9 111.1 %copy-start.2 = (f32[1024]{0:T(1024)}, f32[1024]{0:T(1024)S(1)}, u32[]{:S(2)}) copy-start(f32[1024]{0:T(1024)S(1)} %broadcast_multiply_fusion) | copy-start | bytes 12292
  335.9 67.5 %all-to-all-start.1 = ((bf16[128,8,512]{2,0,1:T(8,128)(2,1)}), bf16[128,8,512]{2,0,1:T(8,128)(2,1)S(1)}, u32[]{:S(2)}, u32[]{:S(2)}) async-start(bf16[128,8,512]{2,0,1:T(8,128)(2,1)} %copy.14), calls=%async_computation.1 | async-start | bytes 2097152 | tf_op jit(solution)/shard_map/all_to_all | solution.py:19
Sparse Core Ops, SparseCore 0:
  10.1 178.6 all-gather.1
  333.1 594.3 reduce-scatter.1
